TPU v7x, 32 devices: a whole 2x2x4 slice. The times are simulated.
32 devices in a mesh: groups: 2 (over y), blk: 4 (over z), split: 2 (over x), sub: 2 (over core).
Axes of the slice: x: 2, y: 2, z: 4, core: 2. Of those that a mesh axis runs over, the one named last changes fastest.
Arguments:
- attention_output_rows: bfloat16 [1024, 8192], P(('groups', 'blk'), 'split'), parts along dimension 0, may hold values from -6 to 6
- residual: bfloat16 [1024, 8192], P(('groups', 'split'), ('blk', 'sub')), parts along dimension 0, may hold values from -6 to 6
- output_projection_weight: bfloat16 [8192, 8192], P('split', ('blk', 'sub')), may hold values from -0.0625 to 0.0625
- down_adapter_bank: bfloat16 [4, 64, 8192], P('blk', None, 'split'), may hold values from -0.0625 to 0.0625
- up_adapter_bank: bfloat16 [4, 64, 8192], P('split', None, ('blk', 'sub')), may hold values from -0.75 to 0.75
- rollout_row_tenant: int32 [1024], P('groups'), parts along dimension 0, may hold values from 0 to 3, as said below
- tenant_bank_entry: int32 [4], replicated, may hold values from 0 to 3, each once
- tenant_live_rank: int32 [4], replicated, may hold values from 16 to 64, as said below
Outputs:
- layer_out: bfloat16 [1024, 8192], P(('groups', 'split'), ('blk', 'sub')), parts along dimension 0
There are 2 independent parts, one for each index of `groups`. A program takes and returns all parts, laid end to end along the dimension named above; an argument that names none is the same for every part. Nothing has to cross between parts.
Inputs may be any that keep to these rules, and one draw needn't show every extreme that they name: `rollout_row_tenant`: every tenant owns at least one row of every part. `tenant_live_rank`: some tenant has the full rank 64.
All inputs are finite; a program needn't handle non-finite values.
Results may differ from a plain program's by a relative error of at most 0.0038.
Values may be sent and summed in bfloat16 or wider, within the bound.
A program may use at most 64 MiB of HBM per device.

v0:
```python
import jax
import jax.numpy as jnp
from jax import lax
from jax.sharding import PartitionSpec as P


def shards(
    attention_output_rows,
    residual,
    output_projection_weight,
    down_adapter_bank,
    up_adapter_bank,
    rollout_row_tenant,
    tenant_bank_entry,
    tenant_live_rank,
):
    out_cols = output_projection_weight.shape[1]
    feat_width = attention_output_rows.shape[1]
    rank_mask_rows = down_adapter_bank.shape[1]
    gathered_down_maps = lax.all_gather(down_adapter_bank, "blk", axis=0, tiled=True)
    tenant_count = gathered_down_maps.shape[0]
    total_rows = rollout_row_tenant.shape[0]
    tenant_ids = jnp.arange(tenant_count, dtype=jnp.int32)
    tenant_hot = (rollout_row_tenant[:, None] == tenant_ids[None, :]).astype(jnp.int32)
    slot_all = jnp.sum(tenant_hot * tenant_bank_entry[None, :], axis=1)
    rank_all = jnp.sum(tenant_hot * tenant_live_rank[None, :], axis=1)
    down_cols = gathered_down_maps.reshape(tenant_count * rank_mask_rows, feat_width).T
    joined = jnp.concatenate([output_projection_weight, down_cols], axis=1)
    own_count = total_rows // lax.axis_size("split")
    own_start = lax.axis_index("split") * own_count
    own_slot = lax.dynamic_slice_in_dim(slot_all, own_start, own_count, 0)
    own_rank = lax.dynamic_slice_in_dim(rank_all, own_start, own_count, 0)
    own_hot = own_slot[:, None] == tenant_ids[None, :]
    full = jnp.dot(
        lax.all_gather(attention_output_rows, "blk", axis=0, tiled=True),
        joined,
        preferred_element_type=jnp.float32,
    )
    piece_hot = slot_all[:, None] == tenant_ids[None, :]
    values = full[:, out_cols:]
    shaped = values.reshape(values.shape[0], tenant_count, rank_mask_rows)
    products = jnp.concatenate(
        [
            full[:, :out_cols],
            jnp.sum(jnp.where(piece_hot[:, :, None], shaped, jnp.zeros((), jnp.float32)), axis=1),
        ],
        axis=1,
    )
    summed = lax.psum_scatter(products, "split", scatter_dimension=0, tiled=True)
    frozen_output_term = summed[:, :out_cols]
    low_rank = summed[:, out_cols:]
    gathered_up_maps = lax.all_gather(up_adapter_bank, "split", axis=0, tiled=True)
    kept_mask = jnp.arange(rank_mask_rows, dtype=jnp.int32)[None, :] < own_rank[:, None]
    scaling = rank_mask_rows / own_rank.astype(jnp.float32)
    low_scaled = jnp.where(
        kept_mask, low_rank * scaling[:, None], jnp.zeros((), jnp.float32)
    ).astype(jnp.bfloat16)
    rank_expanded_rows = jnp.where(
        own_hot[:, :, None], low_scaled[:, None, :], jnp.zeros((), jnp.bfloat16)
    ).reshape(own_count, tenant_count * rank_mask_rows)
    adapter_output_term = jnp.dot(
        rank_expanded_rows,
        gathered_up_maps.reshape(tenant_count * rank_mask_rows, out_cols),
        preferred_element_type=jnp.float32,
    )
    return (residual.astype(jnp.float32) + frozen_output_term + adapter_output_term).astype(
        jnp.bfloat16
    )


def solution(mesh):
    in_specs = (
        P(("groups", "blk"), "split"),
        P(("groups", "split"), ("blk", "sub")),
        P("split", ("blk", "sub")),
        P("blk", None, "split"),
        P("split", None, ("blk", "sub")),
        P("groups"),
        P(),
        P(),
    )
    out_specs = P(("groups", "split"), ("blk", "sub"))
    return jax.shard_map(shards, mesh=mesh, in_specs=in_specs, out_specs=out_specs, check_vma=False)
```

profile of v0, /device:TPU:0, one launch (start us, length us, event | category | flops | bytes accessed | tf_op | source)
XLA Modules:
  0.0 194.9 jit_solution(4081771632402627207)
XLA Ops:
  6.5 0.0 all-gather.3.cloned.1.call-start
  6.5 0.7 all-gather.3.cloned.1.call-update
  7.3 0.0 all-gather.5.cloned.1.call-start
  7.3 0.7 all-gather.5.cloned.1.call-update
  8.0 0.0 reduce-scatter.2.cloned.1.call-start
  8.1 0.8 select_reduce_fusion.1
  8.8 48.5 %all-gather.3.cloned.1.call-done = bf16[4,64,4096]{2,1,0:T(8,128)(2,1)} async-done(((bf16[1,64,4096]{2,1,0:T(8,128)(2,1)}), bf16[4,64,4096]{2,1,0:T(8,128)(2,1)}) %all-gather.3.cloned.1.call-update) | async-done | bytes 2097168 | tf_op jit(solution)/shard_map/all_gather | solution.py:20
  57.3 3.3 %copy.18 = bf16[256,4096]{0,1:T(8,128)(2,1)S(1)} copy(bf16[256,4096]{1,0:T(8,128)(2,1)} %bitcast.14) | data formatting | bytes 4194304 | tf_op jit(solution)/shard_map/reshape | solution.py:27
  60.6 77.9 %all-gather.5.cloned.1.call-done = bf16[512,4096]{1,0:T(8,128)(2,1)} async-done(((bf16[128,4096]{1,0:T(8,128)(2,1)}), bf16[512,4096]{1,0:T(8,128)(2,1)}) %all-gather.5.cloned.1.call-update) | async-done | bytes 4194320 | tf_op jit(solution)/shard_map/all_gather | solution.py:35
  138.5 9.7 %fusion.4 = f32[512,1280]{0,1:T(8,128)S(1)} fusion(bf16[512,4096]{1,0:T(8,128)(2,1)} %all-gather.5.cloned.1.call-done, bf16[4096,256]{1,0:T(8,128)(2,1)S(1)} %bitcast.15, bf16[4096,1024]{1,0:T(8,128)(2,1)} %param.10), kind=kOutput, calls=%fused_computation.4 | convolution fusion | flops 5389680640 | bytes 17301504 | tf_op jit(solution)/shard_map/dot_general | solution.py:34
  148.2 0.2 slice.16
  148.4 0.1 select_reduce_fusion
  148.5 0.0 copy-start
  148.5 1.6 pad_maximum_fusion
  150.0 0.0 copy-start.1
  150.0 0.0 reduce-scatter.2.cloned.1.call-update
  150.1 0.1 dynamic_slice.6
  150.1 0.0 copy-done
  150.1 0.2 copy.17
  150.4 0.1 convert_divide_fusion
  150.4 0.5 copy-done.1
  151.0 12.9 %all_gather.11 = bf16[4,64,1024]{2,1,0:T(8,128)(2,1)S(1)} all-gather(bf16[2,64,1024]{2,1,0:T(8,128)(2,1)S(1)} %copy-done.1), channel_id=1, replica_groups=mesh['groups'=2,'blk'=4,'split'=2,'sub'=2] {'split'}, dimensions={0}, use_global_device_ids=true | all-gather | bytes 786432 | tf_op jit(solution)/shard_map/all_gather | solution.py:52
  163.9 21.1 %reduce-scatter.2.cloned.1.call-done = f32[256,1088]{0,1:T(8,128)} async-done(((f32[512,1088]{0,1:T(8,128)}), f32[256,1088]{0,1:T(8,128)}) %reduce-scatter.2.cloned.1.call-update) | async-done | bytes 1114128 | tf_op jit(solution)/shard_map/reduce_scatter | solution.py:49
  185.0 0.9 fusion.12
  185.8 1.6 fusion.8
  187.4 1.0 copy.20
  (3 shorter events, 0.1 us)
Async XLA Ops:
  6.5 50.8 %all-gather.3.cloned.1.call-start = ((), (), s32[]{:S(2)}) async-start(), calls=%async_computation.1 | async-start | bytes 2621440 | tf_op jit(solution)/shard_map/all_gather | solution.py:20
  7.3 131.2 %all-gather.5.cloned.1.call-start = ((), (), s32[]{:S(2)}) async-start(), calls=%async_computation.2 | async-start | bytes 5242880 | tf_op jit(solution)/shard_map/all_gather | solution.py:35
  8.0 177.0 %reduce-scatter.2.cloned.1.call-start = ((), (), s32[]{:S(2)}) async-start(), calls=%async_computation.3 | async-start | bytes 3342336 | tf_op jit(solution)/shard_map/reduce_scatter | solution.py:49
  148.5 1.7 copy-start
  150.0 0.9 copy-start.1
Sparse Core Ops, SparseCore 0:
  8.9 48.3 all-gather.2
  58.9 79.5 all-gather.4
  150.2 34.7 reduce-scatter.1
where the time goes:
time: 195 us
  waiting for transfers between devices  149 us (76%)
  between operations  13.2 us (7%)
  blocking collectives  12.9 us (7%)
  matrix products  11.3 us (6%)
  local copies, waits for them, and re-layouts  5.31 us (3%)
  other arithmetic  3.35 us (2%)
    all_gather x1, waiting for transfers between devices, shards(): lax.all_gather(attention_output_rows, 'blk', axis=0, tiled=True)  77.9 us
    all_gather x1, waiting for transfers between devices, shards(): lax.all_gather(down_adapter_bank, 'blk', axis=0, tiled=True)  48.5 us
    reduce_scatter x1, waiting for transfers between devices, shards(): lax.psum_scatter(products, 'split', scatter_dimension=0, tiled=True)  21.1 us
    all_gather x1, blocking collectives, shards(): lax.all_gather(up_adapter_bank, 'split', axis=0, tiled=True)  12.9 us
    dot_general x1, matrix products, shards(): jnp.dot(lax.all_gather(attention_output_rows, 'blk', axis=0, tiled=True),...  9.71 us
  transfers between devices with their start and end apart: 3, of which 3 were waited for; matrix products, arithmetic and copies ran while one was open for 2% of the time, Pallas kernels for 0%

commit v1 on v0

--- a/solution.py
+++ b/solution.py
@@ -2,6 +2,28 @@
 import jax.numpy as jnp
 from jax import lax
 from jax.sharding import PartitionSpec as P
+
+
+def in_order(pieces, dim):
+    shape = list(pieces.shape[1:])
+    shape[dim] *= pieces.shape[0]
+    return jnp.moveaxis(pieces, 0, dim).reshape(shape)
+
+
+def gather_around(x, axis, dim):
+    size = lax.axis_size(axis)
+    pairs = [(i, (i + 1) % size) for i in range(size)]
+    back = [(b, a) for a, b in pairs]
+    lower, upper = ([], [])
+    for turn in range(size - 1):
+        if turn % 2 == 0:
+            lower.append(lax.ppermute(lower[-1] if lower else x, axis, pairs))
+        else:
+            upper.append(lax.ppermute(upper[-1] if upper else x, axis, back))
+    blocks = jnp.stack([*lower[::-1], x, *upper])
+    shift = lax.axis_index(axis) - len(lower)
+    blocks = blocks[(jnp.arange(size) - shift) % size]
+    return in_order(blocks, dim)
 
 
 def shards(
@@ -17,7 +39,7 @@
     out_cols = output_projection_weight.shape[1]
     feat_width = attention_output_rows.shape[1]
     rank_mask_rows = down_adapter_bank.shape[1]
-    gathered_down_maps = lax.all_gather(down_adapter_bank, "blk", axis=0, tiled=True)
+    gathered_down_maps = gather_around(down_adapter_bank, "blk", 0)
     tenant_count = gathered_down_maps.shape[0]
     total_rows = rollout_row_tenant.shape[0]
     tenant_ids = jnp.arange(tenant_count, dtype=jnp.int32)

time: 195 us -> 173 us (0.89)
  waiting for transfers between devices: 149 us -> 111 us
  starting transfers between devices: 0.08 us -> 11.8 us
  local copies, waits for them, and re-layouts: 5.31 us -> 7.7 us
    ppermute x0 -> x3, waiting for transfers between devices: none -> 50.6 us  [the longest x1 32.7 us: gather_around(): upper.append(lax.ppermute(upper[-1] if upper else x, axis, back))]
    all_gather x1 -> x0, waiting for transfers between devices: 48.5 us -> none  [shards(): lax.all_gather(down_adapter_bank, 'blk', axis=0, tiled=True)]
    all_gather x1, waiting for transfers between devices: 77.9 us -> 38 us  [shards(): lax.all_gather(attention_output_rows, 'blk', axis=0, tiled=True)]
    ppermute x0 -> x3, starting transfers between devices: none -> 11.8 us  [the longest x2 9.67 us: gather_around(): lower.append(lax.ppermute(lower[-1] if lower else x, axis, pairs))]
    another operation x0 -> x1, local copies, waits for them, and re-layouts: none -> 3.27 us  [shards(): gathered_down_maps.reshape(tenant_count * rank_mask_rows, feat_width)]
    reshape x1 -> x0, local copies, waits for them, and re-layouts: 3.27 us -> none  [shards(): gathered_down_maps.reshape(tenant_count * rank_mask_rows, feat_width)]
    gather x0 -> x1, local copies, waits for them, and re-layouts: none -> 2 us  [gather_around(): blocks = blocks[(jnp.arange(size) - shift) % size]]
  transfers between devices with their start and end apart: 3 -> 5, of which waited for: 3 -> 5; matrix products, arithmetic and copies ran while one was open for 2% -> 4% of each run, Pallas kernels for 0% -> 0%
where the time goes in v1:
time: 173 us
  waiting for transfers between devices  111 us (64%)
  between operations  13.5 us (8%)
  blocking collectives  12.9 us (7%)
  starting transfers between devices  11.8 us (7%)
  matrix products  11.3 us (7%)
  local copies, waits for them, and re-layouts  7.7 us (4%)
  other arithmetic  4.69 us (3%)
    all_gather x1, waiting for transfers between devices, shards(): lax.all_gather(attention_output_rows, 'blk', axis=0, tiled=True)  38 us
    ppermute x1, waiting for transfers between devices, gather_around(): upper.append(lax.ppermute(upper[-1] if upper else x, axis, back))  32.7 us
    reduce_scatter x1, waiting for transfers between devices, shards(): lax.psum_scatter(products, 'split', scatter_dimension=0, tiled=True)  21.4 us
    ppermute x2, waiting for transfers between devices, gather_around(): lower.append(lax.ppermute(lower[-1] if lower else x, axis, pairs))  17.9 us
    all_gather x1, blocking collectives, shards(): lax.all_gather(up_adapter_bank, 'split', axis=0, tiled=True)  12.9 us
    dot_general x1, matrix products, shards(): jnp.dot(lax.all_gather(attention_output_rows, 'blk', axis=0, tiled=True),...  9.71 us
    ppermute x2, starting transfers between devices, gather_around(): lower.append(lax.ppermute(lower[-1] if lower else x, axis, pairs))  9.67 us
  transfers between devices with their start and end apart: 5, of which 5 were waited for; matrix products, arithmetic and copies ran while one was open for 4% of the time, Pallas kernels for 0%

profile of v1, /device:TPU:0, one launch (start us, length us, event | category | flops | bytes accessed | tf_op | source)
XLA Modules:
  0.0 172.6 jit_solution(15908623694549073033)
XLA Ops:
  6.5 0.0 all-gather.2.cloned.1.call-start
  6.5 0.7 all-gather.2.cloned.1.call-update
  7.3 0.0 reduce-scatter.2.cloned.1.call-start
  7.3 3.1 %collective-permute-start = (bf16[1,64,4096]{2,1,0:T(8,128)(2,1)}, bf16[1,64,4096]{2,1,0:T(8,128)(2,1)S(1)}, u32[]{:S(2)}, u32[]{:S(2)}) collective-permute-start(bf16[1,64,4096]{2,1,0:T(8,128)(2,1)} %param.11), channel_id=1, source_target_pairs={{0,4},{4,8},{8,12},{12,0},{1,5},{5,9},{9,13},{13,1},{2,6},{6,10},{... | collective-permute-start | bytes 1572872 | tf_op jit(solution)/shard_map/ppermute | solution.py:20
  10.4 2.1 %collective-permute-start.2 = (bf16[1,64,4096]{2,1,0:T(8,128)(2,1)}, bf16[1,64,4096]{2,1,0:T(8,128)(2,1)S(1)}, u32[]{:S(2)}, u32[]{:S(2)}) collective-permute-start(bf16[1,64,4096]{2,1,0:T(8,128)(2,1)} %param.11), channel_id=1, source_target_pairs={{4,0},{8,4},{12,8},{0,12},{5,1},{9,5},{13,9},{1,13},{6,2},{10,6},{... | collective-permute-start | bytes 1572872 | tf_op jit(solution)/shard_map/ppermute | solution.py:22
  12.5 13.9 %collective-permute-done = bf16[1,64,4096]{2,1,0:T(8,128)(2,1)S(1)} collective-permute-done((bf16[1,64,4096]{2,1,0:T(8,128)(2,1)}, bf16[1,64,4096]{2,1,0:T(8,128)(2,1)S(1)}, u32[]{:S(2)}, u32[]{:S(2)}) %collective-permute-start) | collective-permute-done | bytes 524320 | tf_op jit(solution)/shard_map/ppermute | solution.py:20
  26.4 6.6 %collective-permute-start.1 = (bf16[1,64,4096]{2,1,0:T(8,128)(2,1)S(1)}, bf16[1,64,4096]{2,1,0:T(8,128)(2,1)S(1)}, u32[]{:S(2)}, u32[]{:S(2)}) collective-permute-start(bf16[1,64,4096]{2,1,0:T(8,128)(2,1)S(1)} %collective-permute-done), channel_id=1, source_target_pairs={{0,4},{4,8},{8,12},{12,0},{1,5},{5,9},{9,13},{13,1},{2,6},{6,10},{... | collective-permute-start | bytes 1572872 | tf_op jit(solution)/shard_map/ppermute | solution.py:20
  33.0 0.8 select_reduce_fusion.1
  33.8 32.7 %collective-permute-done.2 = bf16[1,64,4096]{2,1,0:T(8,128)(2,1)S(1)} collective-permute-done((bf16[1,64,4096]{2,1,0:T(8,128)(2,1)}, bf16[1,64,4096]{2,1,0:T(8,128)(2,1)S(1)}, u32[]{:S(2)}, u32[]{:S(2)}) %collective-permute-start.2) | collective-permute-done | bytes 524320 | tf_op jit(solution)/shard_map/ppermute | solution.py:22
  66.5 4.0 %collective-permute-done.1 = bf16[1,64,4096]{2,1,0:T(8,128)(2,1)S(1)} collective-permute-done((bf16[1,64,4096]{2,1,0:T(8,128)(2,1)S(1)}, bf16[1,64,4096]{2,1,0:T(8,128)(2,1)S(1)}, u32[]{:S(2)}, u32[]{:S(2)}) %collective-permute-start.1) | collective-permute-done | bytes 524320 | tf_op jit(solution)/shard_map/ppermute | solution.py:20
  70.5 1.3 maximum_bitcast_fusion
  71.8 2.0 %gather_fusion = bf16[4,64,4096]{2,1,0:T(8,128)(2,1)} fusion(bf16[4,64,4096]{2,1,0:T(8,128)(2,1)S(1)} %maximum_bitcast_fusion, s32[1024]{0:T(1024)S(1)} %pad_clamp_fusion), kind=kCustom, calls=%fused_computation | custom fusion | bytes 4194320 | tf_op jit(solution)/shard_map/gather | solution.py:25
  73.8 3.3 %copy.18 = bf16[256,4096]{0,1:T(8,128)(2,1)S(1)} copy(bf16[256,4096]{1,0:T(8,128)(2,1)} %bitcast.21) | data formatting | bytes 4194304 | tf_op jit(solution)/shard_map/reshape;reshape | solution.py:49
  77.1 38.0 %all-gather.2.cloned.1.call-done = bf16[512,4096]{1,0:T(8,128)(2,1)} async-done(((bf16[128,4096]{1,0:T(8,128)(2,1)}), bf16[512,4096]{1,0:T(8,128)(2,1)}) %all-gather.2.cloned.1.call-update) | async-done | bytes 4194320 | tf_op jit(solution)/shard_map/all_gather | solution.py:57
  115.1 9.7 %fusion.4 = f32[512,1280]{0,1:T(8,128)S(1)} fusion(bf16[512,4096]{1,0:T(8,128)(2,1)} %all-gather.2.cloned.1.call-done, bf16[4096,256]{1,0:T(8,128)(2,1)S(1)} %bitcast.23, bf16[4096,1024]{1,0:T(8,128)(2,1)} %param.10), kind=kOutput, calls=%fused_computation.5 | convolution fusion | flops 5389680640 | bytes 17301504 | tf_op jit(solution)/shard_map/dot_general | solution.py:56
  124.9 0.2 slice.18
  125.0 0.1 select_reduce_fusion
  125.1 1.6 pad_maximum_fusion
  126.7 0.0 copy-start
  126.7 0.0 copy-start.1
  126.7 0.0 reduce-scatter.2.cloned.1.call-update
  126.7 0.1 dynamic_slice.6
  126.8 0.9 copy-done
  127.7 0.2 copy.17
  127.9 0.1 convert_divide_fusion
  128.0 0.0 copy-done.1
  128.0 12.9 %all_gather.7 = bf16[4,64,1024]{2,1,0:T(8,128)(2,1)S(1)} all-gather(bf16[2,64,1024]{2,1,0:T(8,128)(2,1)S(1)} %copy-done.1), channel_id=1, replica_groups=mesh['groups'=2,'blk'=4,'split'=2,'sub'=2] {'split'}, dimensions={0}, use_global_device_ids=true | all-gather | bytes 786432 | tf_op jit(solution)/shard_map/all_gather | solution.py:74
  140.9 21.4 %reduce-scatter.2.cloned.1.call-done = f32[256,1088]{0,1:T(8,128)} async-done(((f32[512,1088]{0,1:T(8,128)}), f32[256,1088]{0,1:T(8,128)}) %reduce-scatter.2.cloned.1.call-update) | async-done | bytes 1114128 | tf_op jit(solution)/shard_map/reduce_scatter | solution.py:71
  162.3 0.9 fusion.12
  163.2 1.6 fusion.8
  164.8 1.0 copy.20
  (5 shorter events, 0.1 us)
Async XLA Ops:
  6.5 108.6 %all-gather.2.cloned.1.call-start = ((), (), s32[]{:S(2)}) async-start(), calls=%async_computation.1 | async-start | bytes 5242880 | tf_op jit(solution)/shard_map/all_gather | solution.py:57
  7.3 155.1 %reduce-scatter.2.cloned.1.call-start = ((), (), s32[]{:S(2)}) async-start(), calls=%async_computation.2 | async-start | bytes 3342336 | tf_op jit(solution)/shard_map/reduce_scatter | solution.py:71
  7.3 19.1 %collective-permute-start = (bf16[1,64,4096]{2,1,0:T(8,128)(2,1)}, bf16[1,64,4096]{2,1,0:T(8,128)(2,1)S(1)}, u32[]{:S(2)}, u32[]{:S(2)}) collective-permute-start(bf16[1,64,4096]{2,1,0:T(8,128)(2,1)} %param.11), channel_id=1, source_target_pairs={{0,4},{4,8},{8,12},{12,0},{1,5},{5,9},{9,13},{13,1},{2,6},{6,10},{... | collective-permute-start | bytes 1572872 | tf_op jit(solution)/shard_map/ppermute | solution.py:20
  10.4 56.1 %collective-permute-start.2 = (bf16[1,64,4096]{2,1,0:T(8,128)(2,1)}, bf16[1,64,4096]{2,1,0:T(8,128)(2,1)S(1)}, u32[]{:S(2)}, u32[]{:S(2)}) collective-permute-start(bf16[1,64,4096]{2,1,0:T(8,128)(2,1)} %param.11), channel_id=1, source_target_pairs={{4,0},{8,4},{12,8},{0,12},{5,1},{9,5},{13,9},{1,13},{6,2},{10,6},{... | collective-permute-start | bytes 1572872 | tf_op jit(solution)/shard_map/ppermute | solution.py:22
  26.4 44.1 %collective-permute-start.1 = (bf16[1,64,4096]{2,1,0:T(8,128)(2,1)S(1)}, bf16[1,64,4096]{2,1,0:T(8,128)(2,1)S(1)}, u32[]{:S(2)}, u32[]{:S(2)}) collective-permute-start(bf16[1,64,4096]{2,1,0:T(8,128)(2,1)S(1)} %collective-permute-done), channel_id=1, source_target_pairs={{0,4},{4,8},{8,12},{12,0},{1,5},{5,9},{9,13},{13,1},{2,6},{6,10},{... | collective-permute-start | bytes 1572872 | tf_op jit(solution)/shard_map/ppermute | solution.py:20
  126.7 1.0 copy-start
  126.7 1.3 copy-start.1
Sparse Core Ops, SparseCore 0:
  8.9 106.1 all-gather.1
  126.8 35.4 reduce-scatter.1
